TPU v7x, 128 devices: a whole 4x4x4 slice. The times are simulated.
128 devices in a mesh: sec: 8 (over z, core), blk: 16 (over y, x).
Axes of the slice: x: 4, y: 4, z: 4, core: 2. Of those that a mesh axis runs over, the one named last changes fastest.
Arguments:
- wavefunction: bfloat16 [8, 192, 128, 128], P('sec', 'blk')
- left_env: bfloat16 [8, 20, 192, 128, 128], P('sec', None, 'blk')
- right_env: bfloat16 [8, 20, 192, 128, 128], P('sec', None, 'blk')
- row_offset: int32 [8, 12], P('sec'), may hold values from 0 to 15, as said below
- sector_dims: int32 [8, 192, 2], P('sec', 'blk'), may hold values from 64 to 128
- trunc_ranks: int32 [8, 192], P('sec', 'blk'), may hold values from 32 to 128
Outputs:
- state_new: bfloat16 [8, 192, 128, 128], P('sec', 'blk')
- hstate_new: bfloat16 [8, 192, 128, 128], P('sec', 'blk')
- energy: float32 [8], P('sec')
- next_left: bfloat16 [8, 20, 192, 128, 128], P('sec', None, 'blk')
Inputs may be any that keep to these rules, and one draw needn't show every extreme that they name: The sector with up-charge u and down-charge e is stored in slot u of device (e + row_offset[u]) mod 16; in every section the offsets of some two adjacent up-charges differ by 16 / 2 modulo 16.
All inputs are finite; a program needn't handle non-finite values.
Results may differ from a plain program's by a relative error of at most 0.0067.
Values may be sent and summed in bfloat16 or wider, within the bound.
A program may use at most 128 MiB of HBM per device.

v0:
```python
import jax
import jax.numpy as jnp
from jax import lax
from jax.sharding import PartitionSpec as P


def passed_along(value, axis, by):
    length = lax.axis_size(axis)
    pairs = [(i, i + by) for i in range(length) if 0 <= i + by < length]
    return lax.ppermute(value, axis, pairs)


def route_blocks(state, offsets, device, nblk):
    count = state.shape[0]
    up_val = jnp.arange(count, dtype=jnp.int32)
    prev_off = jnp.roll(offsets, 1)
    next_off = jnp.roll(offsets, -1)
    down_val = (device - offsets) % nblk
    exists = [up_val >= 1, up_val <= count - 2, down_val >= 1, down_val <= nblk - 2]
    whole = lax.all_gather(state, "blk", axis=0, tiled=True)
    row_lo = jnp.clip(up_val - 1, 0, count - 1)
    row_hi = jnp.clip(up_val + 1, 0, count - 1)
    indices = [
        (down_val + prev_off) % nblk * count + row_lo,
        (down_val + next_off) % nblk * count + row_hi,
        (device - 1) % nblk * count + up_val,
        (device + 1) % nblk * count + up_val,
    ]
    picked = [jnp.take(whole, entry, axis=0) for entry in indices]
    result = [state]
    for ctype in range(4):
        result.append(
            jnp.where(exists[ctype][:, None, None], picked[ctype], jnp.zeros_like(picked[ctype]))
        )
    return result


def apply_ham(state, lenv, renv, mask, offsets, device, nblk):
    blocks = route_blocks(state, offsets, device, nblk)
    total = jnp.zeros(state.shape, jnp.float32)
    for ctype in range(5):
        inner = jnp.einsum(
            "wtab,tbc->wtac", lenv[ctype::5], blocks[ctype], preferred_element_type=jnp.float32
        ).astype(jnp.bfloat16)
        total = total + jnp.einsum(
            "wtac,wtdc->tad", inner, renv[ctype::5], preferred_element_type=jnp.float32
        )
    return total * mask


def shards(wavefunction, left_env, right_env, row_offset, sector_dims, trunc_ranks):
    start = wavefunction[0]
    lenv = left_env[0]
    renv = right_env[0]
    offsets = row_offset[0]
    dims = sector_dims[0]
    kept_cols = trunc_ranks[0]
    count = start.shape[0]
    width = start.shape[1]
    channels = lenv.shape[0]
    nblk = lax.axis_size("blk")
    device = lax.axis_index("blk")
    cells = float(count * nblk * width * width)
    lines = jnp.arange(width, dtype=jnp.int32)
    mask_on = (lines[None, :, None] < dims[:, 0][:, None, None]) & (
        lines[None, None, :] < dims[:, 1][:, None, None]
    )
    mask = mask_on.astype(jnp.float32)
    vzero = jnp.where(mask_on, start, jnp.zeros_like(start))
    hzero = apply_ham(vzero, lenv, renv, mask, offsets, device, nblk)
    vzero_f = vzero.astype(jnp.float32)
    nzero_part = jnp.sum(vzero_f * vzero_f)
    pzero_part = jnp.sum(vzero_f * hzero)
    nzero, pzero = lax.psum((nzero_part, pzero_part), "blk")
    scale = jnp.sqrt(cells / nzero)
    uzero = vzero_f * scale
    huzero = hzero * scale
    a_zero = pzero / nzero
    resid = huzero - a_zero * uzero
    squares = lax.psum(jnp.sum(resid * resid), "blk") / cells
    beta = jnp.sqrt(squares + 1e-06)
    vone = (resid / beta).astype(jnp.bfloat16)
    hone = apply_ham(vone, lenv, renv, mask, offsets, device, nblk)
    a_one = lax.psum(jnp.sum(vone.astype(jnp.float32) * hone), "blk") / cells
    half_gap = (a_zero - a_one) / 2.0
    ritz = (a_zero + a_one) / 2.0 - jnp.sqrt(half_gap * half_gap + beta * beta)
    gap_val = ritz - a_zero
    length = jnp.sqrt(beta * beta + gap_val * gap_val)
    xcoef = beta / length
    ycoef = gap_val / length
    state_new = (xcoef * uzero + ycoef * vone.astype(jnp.float32)).astype(jnp.bfloat16)
    hstate_new = (xcoef * huzero + ycoef * hone).astype(jnp.bfloat16)
    kept_on = lines[None, None, :] < kept_cols[:, None, None]
    kept = jnp.where(kept_on, state_new, jnp.zeros_like(state_new))
    kept_src = route_blocks(kept, offsets, device, nblk)
    pieces = []
    for ctype in range(5):
        inner = jnp.einsum(
            "wtab,tbc->wtac", lenv[ctype::5], kept_src[ctype], preferred_element_type=jnp.float32
        ).astype(jnp.bfloat16)
        piece = jnp.einsum(
            "tba,wtbc->wtac", kept, inner, preferred_element_type=jnp.float32
        ).astype(jnp.bfloat16)
        pieces.append(piece)
    stacked = jnp.stack(pieces, axis=1).reshape((channels, count, width, width))
    received = passed_along(stacked, "sec", 1)
    first_section = lax.axis_index("sec") == 0
    next_left = jnp.where(first_section, lenv, received)
    return (state_new[None], hstate_new[None], jnp.reshape(ritz, (1,)), next_left[None])


def solution(mesh):
    placed = (
        P("sec", "blk", None, None),
        P("sec", None, "blk", None, None),
        P("sec", None, "blk", None, None),
        P("sec", None),
        P("sec", "blk", None),
        P("sec", "blk"),
    )
    return jax.shard_map(
        shards,
        mesh=mesh,
        in_specs=placed,
        out_specs=(
            P("sec", "blk", None, None),
            P("sec", "blk", None, None),
            P("sec"),
            P("sec", None, "blk", None, None),
        ),
        check_vma=False,
    )
```

profile of v0, /device:TPU:1, one launch (start us, length us, event | category | flops | bytes accessed | tf_op | source)
XLA Modules:
  0.0 537.8 jit_solution(6096695522838150606)
XLA Ops:
  8.0 2.0 and_select_fusion
  10.3 1.3 fusion.370
  13.0 1.4 compare_and_fusion.2
  14.5 11.6 %copy_bitcast_fusion = (bf16[20,12,128,128]{3,2,0,1:T(8,128)(2,1)}, bf16[20,12,128,128]{3,2,0,1:T(8,128)(2,1)}) fusion(bf16[1,20,12,128,128]{4,3,2,1,0:T(8,128)(2,1)} %param.10, bf16[1,20,12,128,128]{4,3,2,1,0:T(8,128)(2,1)} %param.9), kind=kLoop, calls=%fused_computation.12 | loop fusion | bytes 31457280 | tf_op jit(solution)/shard_map/squeeze | solution.py:54
  26.0 2.9 fusion.45
  28.9 46.0 %all-gather.4.cloned.1.call-done = bf16[192,128,128]{2,1,0:T(8,128)(2,1)} async-done(((bf16[12,128,128]{2,1,0:T(8,128)(2,1)}), bf16[192,128,128]{2,1,0:T(8,128)(2,1)}) %all-gather.4.cloned.1.call-update) | async-done | bytes 6291472 | tf_op jit(solution)/shard_map/all_gather | solution.py:20
  74.9 3.4 gather_fusion
  78.3 3.4 fusion.140
  81.7 3.4 gather_fusion.1
  85.1 4.3 fusion.135
  89.4 3.4 gather_fusion.2
  92.8 3.6 fusion.130
  96.5 3.4 gather_fusion.3
  99.9 3.9 fusion.181
  103.8 31.8 %all-reduce = (f32[]{:T(128)}, f32[]{:T(128)}) all-reduce(f32[]{:T(128)} %get-tuple-element.10, f32[]{:T(128)} %get-tuple-element.9), channel_id=1, replica_groups=mesh['sec'=8,'blk'=16] {'blk'}, use_global_device_ids=true, to_apply=%region_3.5 | all-reduce | flops 2 | bytes 16 | tf_op jit(solution)/shard_map/psum | solution.py:74
  137.7 0.9 multiply_reduce_fusion
  138.6 29.1 %psum.30 = f32[]{:T(128)} all-reduce(f32[]{:T(128)} %multiply_reduce_fusion), channel_id=1, replica_groups=mesh['sec'=8,'blk'=16] {'blk'}, use_global_device_ids=true, to_apply=%region_5.7 | all-reduce | flops 1 | bytes 8 | tf_op jit(solution)/shard_map/psum | solution.py:80
  168.4 1.1 divide_convert_fusion
  169.9 3.0 fusion.70
  172.9 70.0 %all-gather.6.cloned.1.call-done = bf16[192,128,128]{2,1,0:T(8,128)(2,1)} async-done(((bf16[12,128,128]{2,1,0:T(8,128)(2,1)}), bf16[192,128,128]{2,1,0:T(8,128)(2,1)}) %all-gather.6.cloned.1.call-update) | async-done | bytes 6291472 | tf_op jit(solution)/shard_map/all_gather | solution.py:20
  242.9 3.4 gather_fusion.4
  246.3 4.3 fusion.115
  250.6 3.4 gather_fusion.5
  254.0 3.6 fusion.110
  257.7 3.4 gather_fusion.6
  261.1 4.3 fusion.105
  265.4 3.4 gather_fusion.7
  268.8 4.1 fusion.180
  272.9 32.0 %psum.31 = f32[]{:T(128)} all-reduce(f32[]{:T(128)} %get-tuple-element.29), channel_id=1, replica_groups=mesh['sec'=8,'blk'=16] {'blk'}, use_global_device_ids=true, to_apply=%region_7.9 | all-reduce | flops 1 | bytes 8 | tf_op jit(solution)/shard_map/psum | solution.py:84
  305.7 1.1 broadcast_select_fusion
  306.9 3.8 bitcast_dynamic-update-slice_fusion.4
  310.7 61.1 %all-gather.8.cloned.1.call-done = bf16[192,128,128]{2,1,0:T(8,128)(2,1)} async-done(((bf16[12,128,128]{2,1,0:T(8,128)(2,1)}), bf16[192,128,128]{2,1,0:T(8,128)(2,1)}) %all-gather.8.cloned.1.call-update) | async-done | bytes 6291472 | tf_op jit(solution)/shard_map/all_gather | solution.py:20
  371.8 3.4 gather_fusion.8
  375.2 4.0 bitcast_dynamic-update-slice_fusion.3
  379.2 3.4 gather_fusion.9
  382.6 3.9 bitcast_dynamic-update-slice_fusion.2
  386.5 3.4 gather_fusion.10
  390.0 3.9 bitcast_dynamic-update-slice_fusion.1
  393.9 3.4 gather_fusion.11
  397.3 3.9 bitcast_dynamic-update-slice_fusion
  401.2 10.7 %copy.40 = bf16[4,5,12,128,128]{4,3,2,1,0:T(8,128)(2,1)} copy(bf16[4,5,12,128,128]{3,4,0,2,1:T(8,128)(2,1)} %bitcast_dynamic-update-slice_fusion) | data formatting | bytes 15728640 | tf_op jit(solution)/shard_map/stack | solution.py:105
  411.9 9.9 %copy.41 = bf16[20,12,128,128]{3,2,0,1:T(8,128)(2,1)} copy(bf16[20,12,128,128]{3,2,1,0:T(8,128)(2,1)} %bitcast.313) | data formatting | bytes 15728640 | tf_op jit(solution)/shard_map/reshape | solution.py:105
  421.8 3.9 collective-permute-start
  425.7 1.1 fusion.314
  426.8 0.9 fusion.183
  427.7 83.1 %collective-permute-done = bf16[20,12,128,128]{3,2,0,1:T(8,128)(2,1)} collective-permute-done((bf16[20,12,128,128]{3,2,0,1:T(8,128)(2,1)}, bf16[20,12,128,128]{3,2,0,1:T(8,128)(2,1)}, u32[]{:S(2)}, u32[]{:S(2)}) %collective-permute-start) | collective-permute-done | bytes 7864352 | tf_op jit(solution)/shard_map/ppermute | solution.py:10
  510.8 9.4 %select_bitcast_fusion = bf16[1,20,12,128,128]{4,3,1,2,0:T(8,128)(2,1)} fusion(bf16[20,12,128,128]{3,2,0,1:T(8,128)(2,1)} %collective-permute-done, pred[]{:T(512)S(6)} %eq.20, bf16[1,20,12,128,128]{4,3,2,1,0:T(8,128)(2,1)} %param.9), kind=kLoop, calls=%fused_computation.14 | loop fusion | flops 3932160 | bytes 23592960 | tf_op jit(solution)/shard_map/broadcast_in_dim | solution.py:109
  520.2 9.9 %copy.42 = bf16[1,20,12,128,128]{4,3,2,1,0:T(8,128)(2,1)} copy(bf16[1,20,12,128,128]{4,3,1,2,0:T(8,128)(2,1)} %select_bitcast_fusion) | data formatting | bytes 15728640
  (29 shorter events, 2.8 us)
Async XLA Ops:
  7.2 67.7 %all-gather.4.cloned.1.call-start = ((), (), s32[]{:S(2)}) async-start(), calls=%async_computation | async-start | bytes 6684672 | tf_op jit(solution)/shard_map/all_gather | solution.py:20
  10.1 232.8 %all-gather.6.cloned.1.call-start = ((), (), s32[]{:S(2)}) async-start(), calls=%async_computation.1 | async-start | bytes 6684672 | tf_op jit(solution)/shard_map/all_gather | solution.py:20
  14.4 11.6 %copy-start.2 = (bf16[12,128,128]{2,1,0:T(8,128)(2,1)S(1)}, bf16[12,128,128]{2,1,0:T(8,128)(2,1)}, u32[]{:S(2)}) copy-start(bf16[12,128,128]{2,1,0:T(8,128)(2,1)} %and_select_fusion) | copy-start | bytes 1179652
  92.8 44.9 %copy-start = (bf16[1,12,128,128]{3,2,1,0:T(8,128)(2,1)S(1)}, bf16[1,12,128,128]{3,2,1,0:T(8,128)(2,1)}, u32[]{:S(2)}) copy-start(bf16[1,12,128,128]{3,2,1,0:T(8,128)(2,1)} %param.8) | copy-start | bytes 1179652
  96.5 73.3 %copy-start.4 = (s32[1,12]{1,0:T(1,128)S(1)}, s32[1,12]{1,0:T(1,128)}, u32[]{:S(2)}) copy-start(s32[1,12]{1,0:T(1,128)} %param.13) | copy-start | bytes 148
  169.5 202.3 %all-gather.8.cloned.1.call-start = ((), (), s32[]{:S(2)}) async-start(), calls=%async_computation.2 | async-start | bytes 6684672 | tf_op jit(solution)/shard_map/all_gather | solution.py:20
  254.0 14.8 %copy-start.1 = (bf16[12,128,128]{2,1,0:T(8,128)(2,1)S(1)}, bf16[12,128,128]{2,1,0:T(8,128)(2,1)}, u32[]{:S(2)}) copy-start(bf16[12,128,128]{2,1,0:T(8,128)(2,1)} %divide_convert_fusion) | copy-start | bytes 1179652
  306.8 75.8 %copy-start.3 = (bf16[12,128,128]{2,1,0:T(8,128)(2,1)S(1)}, bf16[12,128,128]{2,1,0:T(8,128)(2,1)}, u32[]{:S(2)}) copy-start(bf16[12,128,128]{2,1,0:T(8,128)(2,1)} %broadcast_select_fusion) | copy-start | bytes 1179652
  421.8 89.0 %collective-permute-start = (bf16[20,12,128,128]{3,2,0,1:T(8,128)(2,1)}, bf16[20,12,128,128]{3,2,0,1:T(8,128)(2,1)}, u32[]{:S(2)}, u32[]{:S(2)}) collective-permute-start(bf16[20,12,128,128]{3,2,0,1:T(8,128)(2,1)} %copy.41), channel_id=1, source_target_pairs={{0,16},{16,32},{32,48},{48,64},{64,80},{80,96},{96,112},{1,17},{17... | collective-permute-start | bytes 23592968 | tf_op jit(solution)/shard_map/ppermute | solution.py:10
Sparse Core Ops, SparseCore 0:
  10.7 64.1 all-gather.3
  169.7 73.1 all-gather.5
  307.0 64.7 all-gather.7
where the time goes:
time: 539 us; the launch traced here: 538 us
  waiting for transfers between devices  260 us (48%)
  blocking collectives  92.9 us (17%)
  local copies, waits for them, and re-layouts  85.8 us (16%)
  matrix products  57.1 us (11%)
  other arithmetic  18.8 us (3%)
  between operations  18.8 us (3%)
    all_gather x3, waiting for transfers between devices, route_blocks(): whole = lax.all_gather(state, 'blk', axis=0, tiled=True)  177 us
    ppermute x1, waiting for transfers between devices, passed_along(): return lax.ppermute(value, axis, pairs)  83.1 us
    gather x12, local copies, waits for them, and re-layouts, route_blocks(): picked = [jnp.take(whole, entry, axis=0) for entry in indices]  40.9 us
    dot_general x10, matrix products, apply_ham(): jnp.einsum('wtac,wtdc->tad', inner, renv[ctype::5], preferred_element_typ...  37.5 us
    psum x1, blocking collectives, shards(): a_one = lax.psum(jnp.sum(vone.astype(jnp.float32) * hone), 'blk') / cells  32 us
    psum x1, blocking collectives, shards(): nzero, pzero = lax.psum((nzero_part, pzero_part), 'blk')  31.8 us
    psum x1, blocking collectives, shards(): squares = lax.psum(jnp.sum(resid * resid), 'blk') / cells  29.1 us
    dot_general x5, matrix products, shards(): jnp.einsum('tba,wtbc->wtac', kept, inner, preferred_element_type=jnp.floa...  19.6 us
  transfers between devices with their start and end apart: 4, of which 4 were waited for; matrix products, arithmetic and copies ran while one was open for 5% of the time, Pallas kernels for 0%

commit v1 on v0

--- a/solution.py
+++ b/solution.py
@@ -17,7 +17,10 @@
     next_off = jnp.roll(offsets, -1)
     down_val = (device - offsets) % nblk
     exists = [up_val >= 1, up_val <= count - 2, down_val >= 1, down_val <= nblk - 2]
-    whole = lax.all_gather(state, "blk", axis=0, tiled=True)
+    local_data_read = lambda slab_in: jnp.concatenate(
+        lax.all_to_all(jnp.stack([slab_in for _ in range(lax.axis_size("blk"))], 0), "blk", 0, 0), 0
+    )
+    whole = local_data_read(state)
     row_lo = jnp.clip(up_val - 1, 0, count - 1)
     row_hi = jnp.clip(up_val + 1, 0, count - 1)
     indices = [

time: 539 us -> 588 us (1.091)
  starting transfers between devices: 4.2 us -> 47.8 us
  between operations: 18.8 us -> 5.51 us
  waiting for transfers between devices: 260 us -> 271 us
    all_to_all x0 -> x3, waiting for transfers between devices: none -> 188 us  [route_blocks(): lax.all_to_all(jnp.stack([slab_in for _ in range(lax.axis_size('blk'))],...]
    all_gather x3 -> x0, waiting for transfers between devices: 177 us -> none  [route_blocks(): whole = lax.all_gather(state, 'blk', axis=0, tiled=True)]
    ppermute x1, starting transfers between devices: 3.9 us -> 30.4 us  [passed_along(): return lax.ppermute(value, axis, pairs)]
    all_to_all x0 -> x3, starting transfers between devices: none -> 17.4 us  [route_blocks(): lax.all_to_all(jnp.stack([slab_in for _ in range(lax.axis_size('blk'))],...]
    another operation x0 -> x3, local copies, waits for them, and re-layouts: none -> 12.7 us  [route_blocks(): jnp.stack([slab_in for _ in range(lax.axis_size('blk'))], 0)]
    squeeze x1 -> x0, local copies, waits for them, and re-layouts: 11.6 us -> none  [shards(): renv = right_env[0]]
    reshape x1 -> x0, local copies, waits for them, and re-layouts: 9.9 us -> none  [shards(): stacked = jnp.stack(pieces, axis=1).reshape((channels, count, width, width))]
    gather x12, local copies, waits for them, and re-layouts: 40.9 us -> 49.9 us  [route_blocks(): picked = [jnp.take(whole, entry, axis=0) for entry in indices]]
  transfers between devices with their start and end apart: 4 -> 4, of which waited for: 4 -> 4; matrix products, arithmetic and copies ran while one was open for 5% -> 6% of each run, Pallas kernels for 0% -> 0%
where the time goes in v1:
time: 588 us; the launch traced here: 587 us
  waiting for transfers between devices  271 us (46%)
  blocking collectives  92.9 us (16%)
  local copies, waits for them, and re-layouts  89.9 us (15%)
  matrix products  59.3 us (10%)
  starting transfers between devices  47.8 us (8%)
  other arithmetic  19.8 us (3%)
    all_to_all x3, waiting for transfers between devices, route_blocks(): lax.all_to_all(jnp.stack([slab_in for _ in range(lax.axis_size('blk'))],...  188 us
    ppermute x1, waiting for transfers between devices, passed_along(): return lax.ppermute(value, axis, pairs)  83.1 us
    gather x12, local copies, waits for them, and re-layouts, route_blocks(): picked = [jnp.take(whole, entry, axis=0) for entry in indices]  49.9 us
    dot_general x10, matrix products, apply_ham(): jnp.einsum('wtac,wtdc->tad', inner, renv[ctype::5], preferred_element_typ...  40.1 us
    psum x1, blocking collectives, shards(): a_one = lax.psum(jnp.sum(vone.astype(jnp.float32) * hone), 'blk') / cells  32.1 us
    psum x1, blocking collectives, shards(): nzero, pzero = lax.psum((nzero_part, pzero_part), 'blk')  31.7 us
    ppermute x1, starting transfers between devices, passed_along(): return lax.ppermute(value, axis, pairs)  30.4 us
    psum x1, blocking collectives, shards(): squares = lax.psum(jnp.sum(resid * resid), 'blk') / cells  29.1 us
  transfers between devices with their start and end apart: 4, of which 4 were waited for; matrix products, arithmetic and copies ran while one was open for 6% of the time, Pallas kernels for 0%

profile of v1, /device:TPU:1, one launch (start us, length us, event | category | flops | bytes accessed | tf_op | source)
XLA Modules:
  0.0 586.6 jit_solution(7495068717136789051)
XLA Ops:
  1.5 1.3 fusion.183
  2.7 4.2 stack.21
  7.0 7.6 %all-to-all-start = ((bf16[16,12,128,128]{3,2,1,0:T(8,128)(2,1)}), bf16[16,12,128,128]{3,2,1,0:T(8,128)(2,1)}, u32[]{:S(2)}, u32[]{:S(2)}) async-start(bf16[16,12,128,128]{3,2,1,0:T(8,128)(2,1)} %stack.21), calls=%async_computation | async-start | bytes 12582912 | tf_op jit(solution)/shard_map/all_to_all | solution.py:21
  14.6 9.9 %copy.93 = bf16[1,20,12,128,128]{4,3,1,2,0:T(8,128)(2,1)} copy(bf16[1,20,12,128,128]{4,3,2,1,0:T(8,128)(2,1)} %param.10) | data formatting | bytes 15728640 | tf_op args[2]
  27.9 2.0 compare_and_fusion.2
  30.5 5.2 fusion.371
  35.7 4.4 fusion.45
  40.1 66.9 %all-to-all-done = bf16[16,12,128,128]{3,2,1,0:T(8,128)(2,1)} async-done(((bf16[16,12,128,128]{3,2,1,0:T(8,128)(2,1)}), bf16[16,12,128,128]{3,2,1,0:T(8,128)(2,1)}, u32[]{:S(2)}, u32[]{:S(2)}) %all-to-all-start) | async-done | bytes 6291488 | tf_op jit(solution)/shard_map/all_to_all | solution.py:21
  107.1 4.1 gather_fusion
  111.2 4.1 gather_fusion.1
  115.3 4.3 gather_fusion.2
  119.6 4.3 gather_fusion.3
  123.9 4.1 fusion.140
  128.0 4.1 fusion.135
  132.2 3.7 fusion.130
  135.8 3.4 fusion.181
  139.3 31.7 %all-reduce = (f32[]{:T(128)}, f32[]{:T(128)}) all-reduce(f32[]{:T(128)} %get-tuple-element.6, f32[]{:T(128)} %get-tuple-element.5), channel_id=1, replica_groups=mesh['sec'=8,'blk'=16] {'blk'}, use_global_device_ids=true, to_apply=%region_3.5 | all-reduce | flops 2 | bytes 16 | tf_op jit(solution)/shard_map/psum | solution.py:77
  174.0 29.1 %psum.30 = f32[]{:T(128)} all-reduce(f32[]{:T(128)} %multiply_reduce_fusion), channel_id=1, replica_groups=mesh['sec'=8,'blk'=16] {'blk'}, use_global_device_ids=true, to_apply=%region_5.7 | all-reduce | flops 1 | bytes 8 | tf_op jit(solution)/shard_map/psum | solution.py:83
  204.1 4.2 stack.22
  208.4 4.9 all-to-all-start.1
  213.4 3.7 fusion.70
  217.2 65.2 %all-to-all-done.1 = bf16[16,12,128,128]{3,2,1,0:T(8,128)(2,1)} async-done(((bf16[16,12,128,128]{3,2,1,0:T(8,128)(2,1)}), bf16[16,12,128,128]{3,2,1,0:T(8,128)(2,1)}, u32[]{:S(2)}, u32[]{:S(2)}) %all-to-all-start.1) | async-done | bytes 6291488 | tf_op jit(solution)/shard_map/all_to_all | solution.py:21
  282.4 4.3 gather_fusion.4
  286.6 4.1 gather_fusion.5
  290.8 4.3 gather_fusion.6
  295.0 3.5 gather_fusion.7
  298.6 4.1 fusion.115
  302.7 4.1 fusion.110
  306.9 4.2 fusion.105
  311.0 4.1 fusion.180
  315.2 32.1 %psum.31 = f32[]{:T(128)} all-reduce(f32[]{:T(128)} %get-tuple-element.30), channel_id=1, replica_groups=mesh['sec'=8,'blk'=16] {'blk'}, use_global_device_ids=true, to_apply=%region_7.9 | all-reduce | flops 1 | bytes 8 | tf_op jit(solution)/shard_map/psum | solution.py:87
  348.4 4.2 stack.24
  352.7 4.9 all-to-all-start.2
  357.5 3.6 bitcast_dynamic-update-slice_fusion.4
  361.1 56.2 %all-to-all-done.2 = bf16[16,12,128,128]{3,2,1,0:T(8,128)(2,1)} async-done(((bf16[16,12,128,128]{3,2,1,0:T(8,128)(2,1)}), bf16[16,12,128,128]{3,2,1,0:T(8,128)(2,1)}, u32[]{:S(2)}, u32[]{:S(2)}) %all-to-all-start.2) | async-done | bytes 6291488 | tf_op jit(solution)/shard_map/all_to_all | solution.py:21
  417.3 4.3 gather_fusion.8
  421.6 4.1 gather_fusion.9
  425.7 4.3 gather_fusion.10
  430.0 4.3 gather_fusion.11
  434.3 4.0 bitcast_dynamic-update-slice_fusion.3
  438.3 4.0 bitcast_dynamic-update-slice_fusion.2
  442.3 4.0 bitcast_dynamic-update-slice_fusion.1
  446.4 3.5 bitcast_dynamic-update-slice_fusion
  449.9 10.7 %copy.12 = bf16[4,5,12,128,128]{4,3,2,1,0:T(8,128)(2,1)} copy(bf16[4,5,12,128,128]{3,4,0,2,1:T(8,128)(2,1)} %bitcast_dynamic-update-slice_fusion) | data formatting | bytes 15728640 | tf_op jit(solution)/shard_map/stack | solution.py:108
  460.5 30.4 %collective-permute-start = (bf16[20,12,128,128]{3,2,1,0:T(8,128)(2,1)}, bf16[20,12,128,128]{3,2,1,0:T(8,128)(2,1)}, u32[]{:S(2)}, u32[]{:S(2)}) collective-permute-start(bf16[20,12,128,128]{3,2,1,0:T(8,128)(2,1)} %bitcast.333), channel_id=1, source_target_pairs={{0,16},{16,32},{32,48},{48,64},{64,80},{80,96},{96,112},{1,17},{17... | collective-permute-start | bytes 23592968 | tf_op jit(solution)/shard_map/ppermute | solution.py:10
  490.9 1.1 fusion.315
  492.9 83.1 %collective-permute-done = bf16[20,12,128,128]{3,2,1,0:T(8,128)(2,1)} collective-permute-done((bf16[20,12,128,128]{3,2,1,0:T(8,128)(2,1)}, bf16[20,12,128,128]{3,2,1,0:T(8,128)(2,1)}, u32[]{:S(2)}, u32[]{:S(2)}) %collective-permute-start) | collective-permute-done | bytes 7864352 | tf_op jit(solution)/shard_map/ppermute | solution.py:10
  576.0 9.5 %select_bitcast_fusion = bf16[1,20,12,128,128]{4,3,2,1,0:T(8,128)(2,1)} fusion(bf16[20,12,128,128]{3,2,1,0:T(8,128)(2,1)} %collective-permute-done, pred[]{:T(512)S(6)} %eq.20, bf16[1,20,12,128,128]{4,3,2,1,0:T(8,128)(2,1)} %param.9), kind=kLoop, calls=%fused_computation.13 | loop fusion | flops 3932160 | bytes 23592960 | tf_op jit(solution)/shard_map/broadcast_in_dim | solution.py:112
  (42 shorter events, 7.4 us)
Async XLA Ops:
  7.0 100.1 %all-to-all-start = ((bf16[16,12,128,128]{3,2,1,0:T(8,128)(2,1)}), bf16[16,12,128,128]{3,2,1,0:T(8,128)(2,1)}, u32[]{:S(2)}, u32[]{:S(2)}) async-start(bf16[16,12,128,128]{3,2,1,0:T(8,128)(2,1)} %stack.21), calls=%async_computation | async-start | bytes 12582912 | tf_op jit(solution)/shard_map/all_to_all | solution.py:21
  14.6 12.0 %copy-start.3 = (s32[1,12]{1,0:T(1,128)S(1)}, s32[1,12]{1,0:T(1,128)}, u32[]{:S(2)}) copy-start(s32[1,12]{1,0:T(1,128)} %param.11) | copy-start | bytes 148
  29.9 77.2 %copy-start.4 = (s32[1024]{0:T(1024)}, s32[1024]{0:T(1024)S(1)}, u32[]{:S(2)}) copy-start(s32[1024]{0:T(1024)S(1)} %get-tuple-element.35) | copy-start | bytes 12292
  30.5 5.2 copy-start
  35.7 96.4 %copy-start.1 = (bf16[4,12,128,128]{3,2,1,0:T(8,128)(2,1)}, bf16[4,12,128,128]{3,2,1,0:T(8,128)(2,1)S(1)}, u32[]{:S(2)}) copy-start(bf16[4,12,128,128]{3,2,1,0:T(8,128)(2,1)S(1)} %get-tuple-element.16) | copy-start | bytes 4718596
  111.2 12.7 %copy-start.9 = (pred[12]{0:T(512)(128)(4,1)S(1)}, pred[12]{0:T(512)(128)(4,1)}, u32[]{:S(2)}) copy-start(pred[12]{0:T(512)(128)(4,1)} %get-tuple-element.23) | copy-start | bytes 40
  128.0 4.1 copy-start.6
  208.4 5.0 copy-start.5
  208.4 74.0 %all-to-all-start.1 = ((bf16[16,12,128,128]{3,2,1,0:T(8,128)(2,1)}), bf16[16,12,128,128]{3,2,1,0:T(8,128)(2,1)}, u32[]{:S(2)}, u32[]{:S(2)}) async-start(bf16[16,12,128,128]{3,2,1,0:T(8,128)(2,1)} %stack.22), calls=%async_computation.1 | async-start | bytes 12582912 | tf_op jit(solution)/shard_map/all_to_all | solution.py:21
  352.7 64.7 %all-to-all-start.2 = ((bf16[16,12,128,128]{3,2,1,0:T(8,128)(2,1)}), bf16[16,12,128,128]{3,2,1,0:T(8,128)(2,1)}, u32[]{:S(2)}, u32[]{:S(2)}) async-start(bf16[16,12,128,128]{3,2,1,0:T(8,128)(2,1)} %stack.24), calls=%async_computation.2 | async-start | bytes 12582912 | tf_op jit(solution)/shard_map/all_to_all | solution.py:21
  417.3 16.9 %copy-start.10 = (pred[12]{0:T(512)(128)(4,1)S(1)}, pred[12]{0:T(512)(128)(4,1)}, u32[]{:S(2)}) copy-start(pred[12]{0:T(512)(128)(4,1)} %get-tuple-element.23) | copy-start | bytes 40
  434.3 4.0 copy-start.8
  438.3 4.0 copy-start.7
  442.3 4.0 copy-start.11
  460.5 31.5 %copy-start.2 = (f32[12,128,128]{2,1,0:T(8,128)S(1)}, f32[12,128,128]{2,1,0:T(8,128)}, u32[]{:S(2)}) copy-start(f32[12,128,128]{2,1,0:T(8,128)} %get-tuple-element.31) | copy-start | bytes 2359300
  460.5 115.4 %collective-permute-start = (bf16[20,12,128,128]{3,2,1,0:T(8,128)(2,1)}, bf16[20,12,128,128]{3,2,1,0:T(8,128)(2,1)}, u32[]{:S(2)}, u32[]{:S(2)}) collective-permute-start(bf16[20,12,128,128]{3,2,1,0:T(8,128)(2,1)} %bitcast.333), channel_id=1, source_target_pairs={{0,16},{16,32},{32,48},{48,64},{64,80},{80,96},{96,112},{1,17},{17... | collective-permute-start | bytes 23592968 | tf_op jit(solution)/shard_map/ppermute | solution.py:10
